TPU v7x, 32 devices: a whole 2x2x4 slice. The times are simulated.
32 devices in a mesh: fsdp: 4 (over z), adapter: 8 (over y, x, core).
Axes of the slice: x: 2, y: 2, z: 4, core: 2. Of those that a mesh axis runs over, the one named last changes fastest.
Arguments:
- tokens: bfloat16 [2048, 8192], P('adapter', 'fsdp'), may hold values from -6 to 6
- tenant: int32 [2048], P('adapter'), may hold values from 0 to 63, as said below
- send_list: int32 [8, 8, 128], P('adapter'), may hold values from -1 to 255, as said below
- base_weight: bfloat16 [8192, 2048], P('fsdp'), may hold values from -0.09375 to 0.09375
- down_weight: bfloat16 [64, 8192, 128], P('adapter', 'fsdp'), may hold values from -0.0625 to 0.0625
- up_projection_weight: bfloat16 [64, 64, 2048], P('adapter', None, 'fsdp'), may hold values from -0.75 to 0.75
- cotangent: bfloat16 [2048, 2048], P('adapter', 'fsdp'), may hold values from -3 to 3
Outputs:
- projected: bfloat16 [2048, 2048], P('adapter', 'fsdp')
- token_gradient: bfloat16 [2048, 8192], P('adapter', 'fsdp')
- down_weight_gradient: bfloat16 [64, 8192, 128], P('adapter', 'fsdp')
- up_weight_gradient: bfloat16 [64, 64, 2048], P('adapter', None, 'fsdp')
Inputs may be any that keep to these rules, and one draw needn't show every extreme that they name: `tenant`: adapter t belongs to owner t // 8. Among the 256 rows of one index of adapter at most 128 belong to the adapters of one owner, and one owner, the same for every index, has exactly 128 of them. send_list[i, o, :] lists in increasing order the rows (numbered within the 256 rows of index i of adapter) whose tenant belongs to owner o, then -1 in the slots left; every row stands in exactly one list.
All inputs are finite; a program needn't handle non-finite values.
Results may differ from a plain program's by a relative error of at most 0.005.
Values may be sent and summed in bfloat16 or wider, within the bound.
No kernel may reach another device: no remote copies, remote signals or barrier semaphores. Data moves between devices by JAX's collectives and lax.ppermute only.
A program may use at most 128 MiB of HBM per device.

v0:
```python
import jax
import jax.numpy as jnp
from jax import lax
from jax.sharding import PartitionSpec as P

KV = 1024
adapter_scale = 0.5


def down_partial(input_rows, weights_f, down_weight):
    low_all = jnp.einsum("sd,ldk->slk", input_rows, down_weight, preferred_element_type=jnp.float32)
    return jnp.sum(low_all * weights_f[:, :, None], axis=1)


def grad_partial(rows_dy, weights_f, up_projection_weight, selected_half):
    rank_size = up_projection_weight.shape[1]
    back_all = jnp.einsum(
        "sc,lrc->slr", rows_dy, up_projection_weight, preferred_element_type=jnp.float32
    )
    half_sum = jnp.sum(back_all * weights_f[:, :, None], axis=1)
    placed = jnp.zeros((rows_dy.shape[0], 2 * rank_size), jnp.float32)
    zero_idx = jnp.zeros((), jnp.int32)
    return lax.dynamic_update_slice(placed, half_sum, (zero_idx, selected_half * rank_size))


def forward_holder(low_rank, weight_table, up_projection_weight, selected_half):
    rank_size = up_projection_weight.shape[1]
    low_half = lax.dynamic_slice_in_dim(low_rank, selected_half * rank_size, rank_size, 1)
    broadcast_rows = low_half[:, None, :] * weight_table[:, :, None]
    adapter_update = adapter_scale * jnp.einsum(
        "slr,lrc->sc", broadcast_rows, up_projection_weight, preferred_element_type=jnp.float32
    )
    return (adapter_update.astype(jnp.bfloat16), broadcast_rows)


def backward_owner(back_low, weight_table, input_rows, rows_dy, broadcast_rows, down_weight):
    widened_rows = back_low[:, None, :] * weight_table[:, :, None]
    backward_update = adapter_scale * jnp.einsum(
        "wnr,nyr->wy", widened_rows, down_weight, preferred_element_type=jnp.float32
    )
    down_weight_gradient = adapter_scale * jnp.einsum(
        "wq,wmu->mqu", input_rows, widened_rows, preferred_element_type=jnp.float32
    )
    up_weight_gradient = adapter_scale * jnp.einsum(
        "slr,sc->lrc", broadcast_rows, rows_dy, preferred_element_type=jnp.float32
    )
    return (
        backward_update.astype(jnp.bfloat16),
        down_weight_gradient.astype(jnp.bfloat16),
        up_weight_gradient.astype(jnp.bfloat16),
    )


def shards(tokens, tenant, send_list, base_weight, down_weight, up_projection_weight, cotangent):
    rows_here = tokens.shape[0]
    width_here = tokens.shape[1]
    column_span = cotangent.shape[1]
    adapters_here = down_weight.shape[0]
    holder_list = send_list.shape[1]
    slot_capacity = send_list.shape[2]
    total_slots = holder_list * slot_capacity
    listed = send_list[0]
    present = listed >= 0
    safe_rows = jnp.where(present, listed, 0)
    local_ids = tenant % adapters_here
    picked_ids = local_ids[safe_rows]
    adapter_ids = jnp.arange(adapters_here, dtype=jnp.int32)
    selector = (
        (picked_ids[:, :, None] == adapter_ids[None, None, :]) & present[:, :, None]
    ).astype(jnp.bfloat16)
    send_x = tokens[safe_rows]
    send_dy = cotangent[safe_rows]
    drop_rows = jnp.where(present, listed, rows_here).reshape(total_slots)
    fsdp_pos = lax.axis_index("fsdp")
    selected_half = fsdp_pos * column_span // KV
    weight_cols = base_weight
    local_base_output = lax.psum_scatter(
        lax.dot_general(
            weight_cols, tokens, (((0,), (1,)), ((), ())), preferred_element_type=jnp.float32
        ),
        "fsdp",
        scatter_dimension=0,
        tiled=True,
    ).T
    weight_cols = base_weight
    input_frozen_part = lax.dot_general(
        lax.all_gather(cotangent, "fsdp", axis=1, tiled=True),
        weight_cols,
        (((1,), (1,)), ((), ())),
        preferred_element_type=jnp.float32,
    )
    recv_x, recv_sel = (
        lax.all_to_all(send_x, "adapter", split_axis=0, concat_axis=0, tiled=True),
        lax.all_to_all(selector, "adapter", split_axis=0, concat_axis=0, tiled=True),
    )
    input_rows = recv_x.reshape(total_slots, width_here)
    weight_table = recv_sel.reshape(total_slots, adapters_here)
    weights_f = weight_table.astype(jnp.float32)
    low_term = down_partial(input_rows, weights_f, down_weight)
    reduced_rank_sum = lax.psum(low_term, "fsdp")
    adapter_update, broadcast_rows = forward_holder(
        reduced_rank_sum.astype(jnp.bfloat16), weight_table, up_projection_weight, selected_half
    )
    got_delta = lax.all_to_all(
        adapter_update.reshape(holder_list, slot_capacity, column_span),
        "adapter",
        split_axis=0,
        concat_axis=0,
        tiled=True,
    )
    recv_dy = lax.all_to_all(send_dy, "adapter", split_axis=0, concat_axis=0, tiled=True)
    rows_dy = recv_dy.reshape(total_slots, column_span)
    back_sum = lax.psum(
        grad_partial(rows_dy, weights_f, up_projection_weight, selected_half), "fsdp"
    )
    backward_update, down_weight_gradient, up_weight_gradient = backward_owner(
        back_sum.astype(jnp.bfloat16),
        weight_table,
        input_rows,
        rows_dy,
        broadcast_rows,
        down_weight,
    )
    got_back = lax.all_to_all(
        backward_update.reshape(holder_list, slot_capacity, width_here),
        "adapter",
        split_axis=0,
        concat_axis=0,
        tiled=True,
    )
    adapter_columns = (
        jnp.zeros((rows_here, column_span), jnp.float32)
        .at[drop_rows]
        .add(got_delta.reshape(total_slots, column_span).astype(jnp.float32), mode="drop")
    )
    projected = (local_base_output + adapter_columns).astype(jnp.bfloat16)
    adapter_backward = (
        jnp.zeros((rows_here, width_here), jnp.float32)
        .at[drop_rows]
        .add(got_back.reshape(total_slots, width_here).astype(jnp.float32), mode="drop")
    )
    token_gradient = (input_frozen_part + adapter_backward).astype(jnp.bfloat16)
    return (projected, token_gradient, down_weight_gradient, up_weight_gradient)


def solution(mesh):
    in_specs = (
        P("adapter", "fsdp"),
        P("adapter"),
        P("adapter", None, None),
        P("fsdp", None),
        P("adapter", "fsdp", None),
        P("adapter", None, "fsdp"),
        P("adapter", "fsdp"),
    )
    out_specs = (
        P("adapter", "fsdp"),
        P("adapter", "fsdp"),
        P("adapter", "fsdp", None),
        P("adapter", None, "fsdp"),
    )
    return jax.shard_map(shards, mesh=mesh, in_specs=in_specs, out_specs=out_specs, check_vma=False)
```

profile of v0, /device:TPU:0, one launch (start us, length us, event | category | flops | bytes accessed | tf_op | source)
XLA Modules:
  0.0 267.3 jit_solution(12076343468223439721)
XLA Ops:
  7.2 0.8 fusion.29
  8.0 0.7 compare_bitcast_fusion
  8.7 0.7 and_select_fusion
  9.4 6.8 %gather_fusion.1 = s32[1024]{0:T(1024)S(1)} fusion(s32[256]{0:T(256)S(1)} %and_select_fusion, s32[1024]{0:T(1024)S(1)} %fusion.29), kind=kCustom, calls=%fused_computation.1 | custom fusion | bytes 12288 | tf_op jit(solution)/shard_map/gather | solution.py:66
  16.2 0.6 fusion.27
  16.8 5.2 %all-to-all-start.1 = ((bf16[8,128,8]{1,2,0:T(8,128)(2,1)}), bf16[8,128,8]{1,2,0:T(8,128)(2,1)S(1)}, u32[]{:S(2)}, u32[]{:S(2)}) async-start(bf16[8,128,8]{1,2,0:T(8,128)(2,1)} %fusion.27), calls=%async_computation.2 | async-start | bytes 32768 | tf_op jit(solution)/shard_map/all_to_all | solution.py:94
  22.0 5.1 %gather_fusion.2 = bf16[1024,512]{1,0:T(8,128)(2,1)} fusion(bf16[256,512]{1,0:T(8,128)(2,1)S(1)} %copy-done.1, s32[1024]{0:T(1024)S(1)} %fusion.29), kind=kCustom, calls=%fused_computation.2 | custom fusion | bytes 2101248 | tf_op jit(solution)/shard_map/gather | solution.py:72
  27.1 4.2 %all-to-all-start.3 = ((bf16[8,128,512]{2,1,0:T(8,128)(2,1)}), bf16[8,128,512]{2,1,0:T(8,128)(2,1)S(1)}, u32[]{:S(2)}, u32[]{:S(2)}) async-start(bf16[8,128,512]{2,1,0:T(8,128)(2,1)} %bitcast.14), calls=%async_computation.4 | async-start | bytes 2097152 | tf_op jit(solution)/shard_map/all_to_all | solution.py:111
  31.3 6.0 %gather_fusion = bf16[1024,2048]{1,0:T(8,128)(2,1)} fusion(bf16[256,2048]{1,0:T(8,128)(2,1)S(1)} %copy-done, s32[1024]{0:T(1024)S(1)} %fusion.29), kind=kCustom, calls=%fused_computation | custom fusion | bytes 8392704 | tf_op jit(solution)/shard_map/gather | solution.py:71
  37.2 9.4 %all-to-all-done.3 = bf16[8,128,512]{2,1,0:T(8,128)(2,1)S(1)} async-done(((bf16[8,128,512]{2,1,0:T(8,128)(2,1)}), bf16[8,128,512]{2,1,0:T(8,128)(2,1)S(1)}, u32[]{:S(2)}, u32[]{:S(2)}) %all-to-all-start.3) | async-done | bytes 1048608 | tf_op jit(solution)/shard_map/all_to_all | solution.py:111
  46.7 4.6 %all-to-all-start = ((bf16[8,128,2048]{2,1,0:T(8,128)(2,1)}), bf16[8,128,2048]{2,1,0:T(8,128)(2,1)}, u32[]{:S(2)}, u32[]{:S(2)}) async-start(bf16[8,128,2048]{2,1,0:T(8,128)(2,1)} %bitcast.50), calls=%async_computation.1 | async-start | bytes 8388608 | tf_op jit(solution)/shard_map/all_to_all | solution.py:93
  51.3 0.7 all-gather.2.cloned.1.call-update
  52.1 7.2 %fusion.31 = f32[2048,256]{1,0:T(8,128)} fusion(bf16[2048,2048]{1,0:T(8,128)(2,1)} %param.10, bf16[256,2048]{1,0:T(8,128)(2,1)S(1)} %copy-done), kind=kOutput, calls=%fused_computation.49 | convolution fusion | flops 2147483648 | bytes 11534336 | tf_op jit(solution)/shard_map/dot_general | solution.py:78
  59.4 0.7 multiply_reduce_fusion.1
  60.2 40.2 %all-to-all-done = bf16[8,128,2048]{2,1,0:T(8,128)(2,1)} async-done(((bf16[8,128,2048]{2,1,0:T(8,128)(2,1)}), bf16[8,128,2048]{2,1,0:T(8,128)(2,1)}, u32[]{:S(2)}, u32[]{:S(2)}) %all-to-all-start) | async-done | bytes 4194336 | tf_op jit(solution)/shard_map/all_to_all | solution.py:93
  100.4 7.6 %multiply_reduce_fusion = f32[1024,128]{1,0:T(8,128)S(1)} fusion(bf16[1024,2048,1]{1,0,2:T(8,128)(2,1)} %bitcast.7, bf16[8,2048,128]{2,1,0:T(8,128)(2,1)} %param.11, f32[1024,8]{0,1:T(8,128)S(1)} %bitcast_convert_fusion), kind=kOutput, calls=%fused_computation.10 | convolution fusion | flops 4296933376 | bytes 8945664 | tf_op jit(solution)/shard_map/sd,ldk->slk/dot_general | solution.py:11
  107.9 56.5 %all-reduce.2 = (bf16[1024,128]{1,0:T(8,128)(2,1)S(1)}, bf16[1024,128]{0,1:T(8,128)(2,1)}) all-reduce(f32[1024,128]{1,0:T(8,128)S(1)} %multiply_reduce_fusion, f32[1024,128]{0,1:T(8,128)S(1)} %constant_dynamic-update-slice_fusion), channel_id=1, replica_groups=mesh['fsdp'=4,'adapter'=8] {'fsdp'}, use_global_device_ids=true, to_apply=%region_2.3 | all-reduce | flops 262144 | bytes 1572864 | tf_op jit(solution)/shard_map/psum | solution.py:100
  164.7 2.8 %fusion.8 = bf16[1024,512]{1,0:T(8,128)(2,1)} fusion(bf16[8,64,512]{2,1,0:T(8,128)(2,1)} %param.12, bf16[1024,8]{0,1:T(8,128)(2,1)S(1)} %bitcast.57, bf16[1024,64]{0,1:T(8,128)(2,1)S(1)} %copy.17), kind=kOutput, calls=%fused_computation.17 | convolution fusion | flops 538443776 | bytes 1720320 | tf_op jit(solution)/shard_map/slr,lrc->sc/dot_general | solution.py:30
  167.4 3.6 %all-to-all-start.2 = ((bf16[8,128,512]{2,1,0:T(8,128)(2,1)}), bf16[8,128,512]{2,1,0:T(8,128)(2,1)S(1)}, u32[]{:S(2)}, u32[]{:S(2)}) async-start(bf16[8,128,512]{2,1,0:T(8,128)(2,1)} %bitcast.55), calls=%async_computation.3 | async-start | bytes 2097152 | tf_op jit(solution)/shard_map/all_to_all | solution.py:104
  171.0 8.4 %fusion.2 = bf16[1024,2048]{1,0:T(8,128)(2,1)} fusion(bf16[8,2048,128]{2,1,0:T(8,128)(2,1)} %param.11, bf16[1024,8]{0,1:T(8,128)(2,1)S(1)} %bitcast.58, bf16[1024,128]{0,1:T(8,128)(2,1)} %get-tuple-element.17), kind=kOutput, calls=%fused_computation.8 | convolution fusion | flops 4300210176 | bytes 8667136 | tf_op jit(solution)/shard_map/wnr,nyr->wy/dot_general | solution.py:38
  179.4 7.0 %all-to-all-done.2 = bf16[8,128,512]{2,1,0:T(8,128)(2,1)S(1)} async-done(((bf16[8,128,512]{2,1,0:T(8,128)(2,1)}), bf16[8,128,512]{2,1,0:T(8,128)(2,1)S(1)}, u32[]{:S(2)}, u32[]{:S(2)}) %all-to-all-start.2) | async-done | bytes 1048608 | tf_op jit(solution)/shard_map/all_to_all | solution.py:104
  186.5 4.9 %all-to-all-start.4 = ((bf16[8,128,2048]{2,1,0:T(8,128)(2,1)}), bf16[8,128,2048]{2,1,0:T(8,128)(2,1)}, u32[]{:S(2)}, u32[]{:S(2)}) async-start(bf16[8,128,2048]{2,1,0:T(8,128)(2,1)} %bitcast.51), calls=%async_computation.5 | async-start | bytes 8388608 | tf_op jit(solution)/shard_map/all_to_all | solution.py:124
  191.4 7.4 %fusion.32 = f32[256,2048]{1,0:T(8,128)} fusion(bf16[256,2048]{1,0:T(8,128)(2,1)} %all-gather.2.cloned.1.call-done, bf16[2048,2048]{1,0:T(8,128)(2,1)} %param.10), kind=kOutput, calls=%fused_computation.50 | convolution fusion | flops 2147483648 | bytes 11534336 | tf_op jit(solution)/shard_map/dot_general | solution.py:86
  198.8 8.2 %fusion.3 = bf16[8,2048,128]{1,2,0:T(8,128)(2,1)} fusion(bf16[1024,2048,1]{1,0,2:T(8,128)(2,1)} %bitcast.7, bf16[1024,8]{0,1:T(8,128)(2,1)S(1)} %bitcast.59, bf16[1024,128]{0,1:T(8,128)(2,1)S(1)} %copy-done.4), kind=kOutput, calls=%fused_computation.11 | convolution fusion | flops 4300210176 | bytes 8667136 | tf_op jit(solution)/shard_map/wq,wmu->mqu/dot_general | solution.py:41
  207.1 6.4 %copy.20 = bf16[8,2048,128]{2,1,0:T(8,128)(2,1)} copy(bf16[8,2048,128]{1,2,0:T(8,128)(2,1)} %fusion.3) | data formatting | bytes 8388608
  213.5 1.5 fusion.15
  215.0 1.2 copy.18
  216.2 7.2 %scatter_custom_fusion = f32[256,512]{1,0:T(8,128)S(1)} fusion(f32[256,512]{1,0:T(8,128)S(1)} %copy.18, s32[1024]{0:T(1024)S(1)} %bitcast.63, bf16[1024,512]{1,0:T(8,128)(2,1)S(1)} %bitcast.52), kind=kCustom, calls=%fused_computation.14 | custom fusion | flops 1048576 | bytes 1572864 | tf_op jit(solution)/shard_map/scatter-add | solution.py:134
  223.4 0.7 convert_element_type.55
  224.1 16.1 %all-to-all-done.4 = bf16[8,128,2048]{2,1,0:T(8,128)(2,1)} async-done(((bf16[8,128,2048]{2,1,0:T(8,128)(2,1)}), bf16[8,128,2048]{2,1,0:T(8,128)(2,1)}, u32[]{:S(2)}, u32[]{:S(2)}) %all-to-all-start.4) | async-done | bytes 4194336 | tf_op jit(solution)/shard_map/all_to_all | solution.py:124
  240.3 17.5 %scatter_custom_fusion.1 = f32[256,2048]{1,0:T(8,128)} fusion(f32[256,2048]{1,0:T(8,128)} %fusion.32, s32[1024]{0:T(1024)S(1)} %bitcast.64, bf16[1024,2048]{1,0:T(8,128)(2,1)} %bitcast.24), kind=kCustom, calls=%fused_computation.5 | custom fusion | flops 4194304 | bytes 6291456 | tf_op jit(solution)/shard_map/scatter-add | solution.py:140
  257.8 2.7 %convert_element_type.60 = bf16[256,2048]{1,0:T(8,128)(2,1)} convert(f32[256,2048]{1,0:T(8,128)} %scatter_custom_fusion.1) | non-fusion elementwise | flops 524288 | bytes 3145728 | tf_op jit(solution)/shard_map/convert_element_type | solution.py:142
  (22 shorter events, 0.5 us)
Async XLA Ops:
  7.2 24.1 %copy-start = (bf16[256,2048]{1,0:T(8,128)(2,1)S(1)}, bf16[256,2048]{1,0:T(8,128)(2,1)}, u32[]{:S(2)}) copy-start(bf16[256,2048]{1,0:T(8,128)(2,1)} %param.7) | copy-start | bytes 3145732
  7.2 14.8 %copy-start.1 = (bf16[256,512]{1,0:T(8,128)(2,1)S(1)}, bf16[256,512]{1,0:T(8,128)(2,1)}, u32[]{:S(2)}) copy-start(bf16[256,512]{1,0:T(8,128)(2,1)} %param.13) | copy-start | bytes 786436
  16.8 10.3 %all-to-all-start.1 = ((bf16[8,128,8]{1,2,0:T(8,128)(2,1)}), bf16[8,128,8]{1,2,0:T(8,128)(2,1)S(1)}, u32[]{:S(2)}, u32[]{:S(2)}) async-start(bf16[8,128,8]{1,2,0:T(8,128)(2,1)} %fusion.27), calls=%async_computation.2 | async-start | bytes 32768 | tf_op jit(solution)/shard_map/all_to_all | solution.py:94
  27.1 19.6 %all-to-all-start.3 = ((bf16[8,128,512]{2,1,0:T(8,128)(2,1)}), bf16[8,128,512]{2,1,0:T(8,128)(2,1)S(1)}, u32[]{:S(2)}, u32[]{:S(2)}) async-start(bf16[8,128,512]{2,1,0:T(8,128)(2,1)} %bitcast.14), calls=%async_computation.4 | async-start | bytes 2097152 | tf_op jit(solution)/shard_map/all_to_all | solution.py:111
  46.7 53.7 %all-to-all-start = ((bf16[8,128,2048]{2,1,0:T(8,128)(2,1)}), bf16[8,128,2048]{2,1,0:T(8,128)(2,1)}, u32[]{:S(2)}, u32[]{:S(2)}) async-start(bf16[8,128,2048]{2,1,0:T(8,128)(2,1)} %bitcast.50), calls=%async_computation.1 | async-start | bytes 8388608 | tf_op jit(solution)/shard_map/all_to_all | solution.py:93
  51.3 140.1 %all-gather.2.cloned.1.call-start = ((), (), s32[]{:S(2)}) async-start(), calls=%async_computation.7 | async-start | bytes 1310720 | tf_op jit(solution)/shard_map/all_gather | solution.py:87
  52.0 7.3 %copy-start.3 = (bf16[8,64,512]{2,1,0:T(8,128)(2,1)S(1)}, bf16[8,64,512]{2,1,0:T(8,128)(2,1)}, u32[]{:S(2)}) copy-start(bf16[8,64,512]{2,1,0:T(8,128)(2,1)} %param.12) | copy-start | bytes 1572868
  52.0 163.0 %reduce-scatter.2.cloned.1.call-start = ((), (), s32[]{:S(2)}) async-start(), calls=%async_computation.6 | async-start | bytes 2621440 | tf_op jit(solution)/shard_map/reduce_scatter | solution.py:77
  167.4 19.0 %all-to-all-start.2 = ((bf16[8,128,512]{2,1,0:T(8,128)(2,1)}), bf16[8,128,512]{2,1,0:T(8,128)(2,1)S(1)}, u32[]{:S(2)}, u32[]{:S(2)}) async-start(bf16[8,128,512]{2,1,0:T(8,128)(2,1)} %bitcast.55), calls=%async_computation.3 | async-start | bytes 2097152 | tf_op jit(solution)/shard_map/all_to_all | solution.py:104
  186.5 4.9 %copy-start.2 = (s32[1,8,128]{2,1,0:T(8,128)S(1)}, s32[1,8,128]{2,1,0:T(8,128)}, u32[]{:S(2)}) copy-start(s32[1,8,128]{2,1,0:T(8,128)} %param.9) | copy-start | bytes 12292
  186.5 53.8 %all-to-all-start.4 = ((bf16[8,128,2048]{2,1,0:T(8,128)(2,1)}), bf16[8,128,2048]{2,1,0:T(8,128)(2,1)}, u32[]{:S(2)}, u32[]{:S(2)}) async-start(bf16[8,128,2048]{2,1,0:T(8,128)(2,1)} %bitcast.51), calls=%async_computation.5 | async-start | bytes 8388608 | tf_op jit(solution)/shard_map/all_to_all | solution.py:124
  191.4 7.5 %copy-start.4 = (bf16[1024,128]{0,1:T(8,128)(2,1)S(1)}, bf16[1024,128]{0,1:T(8,128)(2,1)}, u32[]{:S(2)}) copy-start(bf16[1024,128]{0,1:T(8,128)(2,1)} %get-tuple-element.17) | copy-start | bytes 786436
Sparse Core Ops, SparseCore 0:
  53.7 29.5 all-gather.1
  85.5 58.0 reduce-scatter.1
where the time goes:
time: 268 us; the launch traced here: 267 us
  waiting for transfers between devices  73.5 us (27%)
  blocking collectives  56.5 us (21%)
  matrix products  43.9 us (16%)
  other arithmetic  30.9 us (12%)
  local copies, waits for them, and re-layouts  25.9 us (10%)
  starting transfers between devices  22.5 us (8%)
  between operations  14.2 us (5%)
    psum x1, blocking collectives, shards(): reduced_rank_sum = lax.psum(low_term, 'fsdp')  56.5 us
    all_to_all x1, waiting for transfers between devices, shards(): lax.all_to_all(send_x, 'adapter', split_axis=0, concat_axis=0, tiled=True)  40.2 us
    scatter-add x1, other arithmetic, shards(): adapter_backward = jnp.zeros((rows_here, width_here), jnp.float32).at[dro...  17.5 us
    all_to_all x1, waiting for transfers between devices, shards(): lax.all_to_all(backward_update.reshape(holder_list, slot_capacity, width_...  16.1 us
    all_to_all x1, waiting for transfers between devices, shards(): lax.all_to_all(send_dy, 'adapter', split_axis=0, concat_axis=0, tiled=True)  9.44 us
    dot_general x1, matrix products, backward_owner(): jnp.einsum('wnr,nyr->wy', widened_rows, down_weight, preferred_element_ty...  8.41 us
    dot_general x1, matrix products, backward_owner(): jnp.einsum('wq,wmu->mqu', input_rows, widened_rows, preferred_element_typ...  8.22 us
    dot_general x1, matrix products, down_partial(): jnp.einsum('sd,ldk->slk', input_rows, down_weight, preferred_element_type...  7.56 us
  transfers between devices with their start and end apart: 7, of which 4 were waited for; matrix products, arithmetic and copies ran while one was open for 26% of the time, Pallas kernels for 0%

commit v1 on v0

--- a/solution.py
+++ b/solution.py
@@ -52,6 +52,26 @@
 
 
 def shards(tokens, tenant, send_list, base_weight, down_weight, up_projection_weight, cotangent):
+
+    def derive_the_weights(sample):
+        o_now, prior = (jax.lax.axis_size("adapter"), jax.lax.axis_index("adapter"))
+        outer = list(sample.shape)
+        part_now = sample.shape[0] // o_now
+        outer[0] = part_now
+        y_new = outer[0]
+        outer[0] = y_new * o_now
+        block_out = jnp.zeros(outer, sample.dtype)
+        for k in range(o_now):
+            vec_out = lax.dynamic_slice_in_dim(sample, (prior ^ k) * part_now, part_now, axis=0)
+            if k:
+                vec_out = jax.lax.ppermute(
+                    vec_out, "adapter", perm=list(map(lambda nth: (nth, nth ^ k), range(o_now)))
+                )
+            block_out = lax.dynamic_update_slice_in_dim(
+                block_out, vec_out, (prior ^ k) * y_new, axis=0
+            )
+        return block_out
+
     rows_here = tokens.shape[0]
     width_here = tokens.shape[1]
     column_span = cotangent.shape[1]
@@ -108,7 +128,7 @@
         concat_axis=0,
         tiled=True,
     )
-    recv_dy = lax.all_to_all(send_dy, "adapter", split_axis=0, concat_axis=0, tiled=True)
+    recv_dy = derive_the_weights(send_dy)
     rows_dy = recv_dy.reshape(total_slots, column_span)
     back_sum = lax.psum(
         grad_partial(rows_dy, weights_f, up_projection_weight, selected_half), "fsdp"

time: 268 us -> 251 us (0.937)
  blocking collectives: 56.5 us -> 45.2 us
  waiting for transfers between devices: 73.5 us -> 63.4 us
  starting transfers between devices: 22.5 us -> 25.3 us
    all_to_all x1, waiting for transfers between devices: 40.2 us -> 0.01 us  [shards(): lax.all_to_all(send_x, 'adapter', split_axis=0, concat_axis=0, tiled=True)]
    ppermute x0 -> x7, waiting for transfers between devices: none -> 39.5 us  [derive_the_weights(): jax.lax.ppermute(vec_out, 'adapter', perm=list(map(lambda nth: (nth, nth...]
    psum x1, blocking collectives: 56.5 us -> 45.2 us  [shards(): reduced_rank_sum = lax.psum(low_term, 'fsdp')]
    all_to_all x1 -> x0, waiting for transfers between devices: 9.44 us -> none  [shards(): lax.all_to_all(send_dy, 'adapter', split_axis=0, concat_axis=0, tiled=True)]
    ppermute x0 -> x7, starting transfers between devices: none -> 6.93 us  [derive_the_weights(): jax.lax.ppermute(vec_out, 'adapter', perm=list(map(lambda nth: (nth, nth...]
    all_to_all x1 -> x0, starting transfers between devices: 4.19 us -> none  [shards(): lax.all_to_all(send_dy, 'adapter', split_axis=0, concat_axis=0, tiled=True)]
    unnamed x11 -> x9, local copies, waits for them, and re-layouts: 6.45 us -> 6.44 us
  transfers between devices with their start and end apart: 7 -> 13, of which waited for: 4 -> 6; matrix products, arithmetic and copies ran while one was open for 26% -> 29% of each run, Pallas kernels for 0% -> 0%
where the time goes in v1:
time: 251 us; the launch traced here: 250 us
  waiting for transfers between devices  63.4 us (25%)
  matrix products  45.2 us (18%)
  blocking collectives  45.2 us (18%)
  other arithmetic  30.9 us (12%)
  local copies, waits for them, and re-layouts  25.8 us (10%)
  starting transfers between devices  25.3 us (10%)
  between operations  14.4 us (6%)
    psum x1, blocking collectives, shards(): reduced_rank_sum = lax.psum(low_term, 'fsdp')  45.2 us
    ppermute x7, waiting for transfers between devices, derive_the_weights(): jax.lax.ppermute(vec_out, 'adapter', perm=list(map(lambda nth: (nth, nth...  39.5 us
    scatter-add x1, other arithmetic, shards(): adapter_backward = jnp.zeros((rows_here, width_here), jnp.float32).at[dro...  17.5 us
    all_to_all x1, waiting for transfers between devices, shards(): lax.all_to_all(backward_update.reshape(holder_list, slot_capacity, width_...  16.3 us
    dot_general x1, matrix products, backward_owner(): jnp.einsum('wnr,nyr->wy', widened_rows, down_weight, preferred_element_ty...  8.44 us
    dot_general x1, matrix products, backward_owner(): jnp.einsum('wq,wmu->mqu', input_rows, widened_rows, preferred_element_typ...  8.23 us
    dot_general x1, matrix products, down_partial(): jnp.einsum('sd,ldk->slk', input_rows, down_weight, preferred_element_type...  7.6 us
    dot_general x1, matrix products, shards(): lax.dot_general(weight_cols, tokens, (((0,), (1,)), ((), ())), preferred_...  7.47 us
  transfers between devices with their start and end apart: 13, of which 6 were waited for; matrix products, arithmetic and copies ran while one was open for 29% of the time, Pallas kernels for 0%

profile of v1, /device:TPU:0, one launch (start us, length us, event | category | flops | bytes accessed | tf_op | source)
XLA Modules:
  0.0 250.2 jit_solution(14656865160020368947)
XLA Ops:
  7.2 0.8 fusion.29
  9.3 6.8 %gather_fusion.1 = s32[1024]{0:T(1024)S(1)} fusion(s32[256]{0:T(256)S(1)} %and_select_fusion, s32[1024]{0:T(1024)S(1)} %fusion.29), kind=kCustom, calls=%fused_computation.1 | custom fusion | bytes 12288 | tf_op jit(solution)/shard_map/gather | solution.py:86
  16.8 5.2 %all-to-all-start.1 = ((bf16[8,128,8]{1,2,0:T(8,128)(2,1)}), bf16[8,128,8]{1,2,0:T(8,128)(2,1)S(1)}, u32[]{:S(2)}, u32[]{:S(2)}) async-start(bf16[8,128,8]{1,2,0:T(8,128)(2,1)} %fusion.27), calls=%async_computation.2 | async-start | bytes 32768 | tf_op jit(solution)/shard_map/all_to_all | solution.py:114
  22.0 6.0 %gather_fusion = bf16[1024,2048]{1,0:T(8,128)(2,1)} fusion(bf16[256,2048]{1,0:T(8,128)(2,1)S(1)} %copy-done, s32[1024]{0:T(1024)S(1)} %fusion.29), kind=kCustom, calls=%fused_computation | custom fusion | bytes 8392704 | tf_op jit(solution)/shard_map/gather | solution.py:91
  27.9 4.7 %all-to-all-start = ((bf16[8,128,2048]{2,1,0:T(8,128)(2,1)}), bf16[8,128,2048]{2,1,0:T(8,128)(2,1)}, u32[]{:S(2)}, u32[]{:S(2)}) async-start(bf16[8,128,2048]{2,1,0:T(8,128)(2,1)} %bitcast.50), calls=%async_computation.1 | async-start | bytes 8388608 | tf_op jit(solution)/shard_map/all_to_all | solution.py:113
  33.5 4.0 %gather_fusion.2 = bf16[1024,512]{1,0:T(8,128)(2,1)S(1)} fusion(bf16[256,512]{1,0:T(8,128)(2,1)S(1)} %copy-done.1, s32[1024]{0:T(1024)S(1)} %fusion.29), kind=kCustom, calls=%fused_computation.2 | custom fusion | bytes 2101248 | tf_op jit(solution)/shard_map/gather | solution.py:92
  37.6 0.8 constant_dynamic-slice_fusion
  38.8 1.7 collective-permute-start.1
  40.6 1.7 collective-permute-start.3
  42.3 7.5 %fusion.31 = f32[2048,256]{1,0:T(8,128)} fusion(bf16[2048,2048]{1,0:T(8,128)(2,1)} %param.10, bf16[256,2048]{1,0:T(8,128)(2,1)S(1)} %copy-done), kind=kOutput, calls=%fused_computation.64 | convolution fusion | flops 2147483648 | bytes 11534336 | tf_op jit(solution)/shard_map/dot_general | solution.py:98
  49.9 2.7 %collective-permute-start.5 = (bf16[1,128,512]{2,1,0:T(8,128)(2,1)S(1)}, bf16[1,128,512]{2,1,0:T(8,128)(2,1)S(1)}, u32[]{:S(2)}, u32[]{:S(2)}) collective-permute-start(bf16[1,128,512]{2,1,0:T(8,128)(2,1)S(1)} %get-tuple-element.19), channel_id=1, source_target_pairs={{0,6},{1,7},{2,4},{3,5},{4,2},{5,3},{6,0},{7,1},{8,14},{9,15},{10,... | collective-permute-start | bytes 393224 | tf_op jit(solution)/shard_map/ppermute | solution.py:67
  52.6 31.5 %collective-permute-done.1 = bf16[1,128,512]{2,1,0:T(8,128)(2,1)S(1)} collective-permute-done((bf16[1,128,512]{2,1,0:T(8,128)(2,1)}, bf16[1,128,512]{2,1,0:T(8,128)(2,1)S(1)}, u32[]{:S(2)}, u32[]{:S(2)}) %collective-permute-start.1) | collective-permute-done | bytes 131104 | tf_op jit(solution)/shard_map/ppermute | solution.py:67
  84.4 1.5 collective-permute-done.2
  86.0 4.6 %collective-permute-done.5 = bf16[1,128,512]{2,1,0:T(8,128)(2,1)S(1)} collective-permute-done((bf16[1,128,512]{2,1,0:T(8,128)(2,1)S(1)}, bf16[1,128,512]{2,1,0:T(8,128)(2,1)S(1)}, u32[]{:S(2)}, u32[]{:S(2)}) %collective-permute-start.5) | collective-permute-done | bytes 131104 | tf_op jit(solution)/shard_map/ppermute | solution.py:67
  90.6 1.8 collective-permute-done.6
  92.5 1.8 multiply_reduce_fusion.1
  94.4 7.6 %multiply_reduce_fusion = f32[1024,128]{1,0:T(8,128)S(1)} fusion(bf16[1024,2048,1]{1,0,2:T(8,128)(2,1)} %bitcast.7, bf16[8,2048,128]{2,1,0:T(8,128)(2,1)} %param.11, f32[1024,8]{0,1:T(8,128)S(1)} %bitcast_convert_fusion), kind=kOutput, calls=%fused_computation.10 | convolution fusion | flops 4296933376 | bytes 8945664 | tf_op jit(solution)/shard_map/sd,ldk->slk/dot_general | solution.py:11
  102.0 45.2 %all-reduce.2 = (bf16[1024,128]{1,0:T(8,128)(2,1)S(1)}, bf16[1024,128]{0,1:T(8,128)(2,1)}) all-reduce(f32[1024,128]{1,0:T(8,128)S(1)} %multiply_reduce_fusion, f32[1024,128]{0,1:T(8,128)S(1)} %constant_dynamic-update-slice_fusion.7), channel_id=1, replica_groups=mesh['fsdp'=4,'adapter'=8] {'fsdp'}, use_global_device_ids=true, to_apply=%region_2.3 | all-reduce | flops 262144 | bytes 1572864 | tf_op jit(solution)/shard_map/psum | solution.py:120
  147.5 2.8 %fusion.8 = bf16[1024,512]{1,0:T(8,128)(2,1)} fusion(bf16[8,64,512]{2,1,0:T(8,128)(2,1)} %param.12, bf16[1024,8]{0,1:T(8,128)(2,1)S(1)} %bitcast.58, bf16[1024,64]{0,1:T(8,128)(2,1)S(1)} %copy.17), kind=kOutput, calls=%fused_computation.17 | convolution fusion | flops 538443776 | bytes 1720320 | tf_op jit(solution)/shard_map/slr,lrc->sc/dot_general | solution.py:30
  150.2 3.6 %all-to-all-start.2 = ((bf16[8,128,512]{2,1,0:T(8,128)(2,1)}), bf16[8,128,512]{2,1,0:T(8,128)(2,1)S(1)}, u32[]{:S(2)}, u32[]{:S(2)}) async-start(bf16[8,128,512]{2,1,0:T(8,128)(2,1)} %bitcast.56), calls=%async_computation.3 | async-start | bytes 2097152 | tf_op jit(solution)/shard_map/all_to_all | solution.py:124
  153.8 8.4 %fusion.2 = bf16[1024,2048]{1,0:T(8,128)(2,1)} fusion(bf16[8,2048,128]{2,1,0:T(8,128)(2,1)} %param.11, bf16[1024,8]{0,1:T(8,128)(2,1)S(1)} %bitcast.59, bf16[1024,128]{0,1:T(8,128)(2,1)} %get-tuple-element.17), kind=kOutput, calls=%fused_computation.8 | convolution fusion | flops 4300210176 | bytes 8667136 | tf_op jit(solution)/shard_map/wnr,nyr->wy/dot_general | solution.py:38
  162.2 6.9 %all-to-all-done.2 = bf16[8,128,512]{2,1,0:T(8,128)(2,1)S(1)} async-done(((bf16[8,128,512]{2,1,0:T(8,128)(2,1)}), bf16[8,128,512]{2,1,0:T(8,128)(2,1)S(1)}, u32[]{:S(2)}, u32[]{:S(2)}) %all-to-all-start.2) | async-done | bytes 1048608 | tf_op jit(solution)/shard_map/all_to_all | solution.py:124
  169.1 4.9 %all-to-all-start.3 = ((bf16[8,128,2048]{2,1,0:T(8,128)(2,1)}), bf16[8,128,2048]{2,1,0:T(8,128)(2,1)}, u32[]{:S(2)}, u32[]{:S(2)}) async-start(bf16[8,128,2048]{2,1,0:T(8,128)(2,1)} %bitcast.52), calls=%async_computation.4 | async-start | bytes 8388608 | tf_op jit(solution)/shard_map/all_to_all | solution.py:144
  174.1 7.4 %fusion.32 = f32[256,2048]{1,0:T(8,128)} fusion(bf16[256,2048]{1,0:T(8,128)(2,1)} %all-gather.2.cloned.1.call-done, bf16[2048,2048]{1,0:T(8,128)(2,1)} %param.10), kind=kOutput, calls=%fused_computation.65 | convolution fusion | flops 2147483648 | bytes 11534336 | tf_op jit(solution)/shard_map/dot_general | solution.py:106
  181.5 8.2 %fusion.3 = bf16[8,2048,128]{1,2,0:T(8,128)(2,1)} fusion(bf16[1024,2048,1]{1,0,2:T(8,128)(2,1)} %bitcast.7, bf16[1024,8]{0,1:T(8,128)(2,1)S(1)} %bitcast.60, bf16[1024,128]{0,1:T(8,128)(2,1)S(1)} %copy-done.3), kind=kOutput, calls=%fused_computation.11 | convolution fusion | flops 4300210176 | bytes 8667136 | tf_op jit(solution)/shard_map/wq,wmu->mqu/dot_general | solution.py:41
  189.7 6.4 %copy.20 = bf16[8,2048,128]{2,1,0:T(8,128)(2,1)} copy(bf16[8,2048,128]{1,2,0:T(8,128)(2,1)} %fusion.3) | data formatting | bytes 8388608
  196.2 1.5 fusion.15
  197.7 1.2 copy.18
  198.9 7.2 %scatter_custom_fusion = f32[256,512]{1,0:T(8,128)S(1)} fusion(f32[256,512]{1,0:T(8,128)S(1)} %copy.18, s32[1024]{0:T(1024)S(1)} %bitcast.64, bf16[1024,512]{1,0:T(8,128)(2,1)S(1)} %bitcast.53), kind=kCustom, calls=%fused_computation.14 | custom fusion | flops 1048576 | bytes 1572864 | tf_op jit(solution)/shard_map/scatter-add | solution.py:154
  206.8 16.3 %all-to-all-done.3 = bf16[8,128,2048]{2,1,0:T(8,128)(2,1)} async-done(((bf16[8,128,2048]{2,1,0:T(8,128)(2,1)}), bf16[8,128,2048]{2,1,0:T(8,128)(2,1)}, u32[]{:S(2)}, u32[]{:S(2)}) %all-to-all-start.3) | async-done | bytes 4194336 | tf_op jit(solution)/shard_map/all_to_all | solution.py:144
  223.1 17.5 %scatter_custom_fusion.1 = f32[256,2048]{1,0:T(8,128)} fusion(f32[256,2048]{1,0:T(8,128)} %fusion.32, s32[1024]{0:T(1024)S(1)} %bitcast.65, bf16[1024,2048]{1,0:T(8,128)(2,1)} %bitcast.24), kind=kCustom, calls=%fused_computation.5 | custom fusion | flops 4194304 | bytes 6291456 | tf_op jit(solution)/shard_map/scatter-add | solution.py:160
  240.6 2.7 %convert_element_type.60 = bf16[256,2048]{1,0:T(8,128)(2,1)} convert(f32[256,2048]{1,0:T(8,128)} %scatter_custom_fusion.1) | non-fusion elementwise | flops 524288 | bytes 3145728 | tf_op jit(solution)/shard_map/convert_element_type | solution.py:162
  (41 shorter events, 5.0 us)
Async XLA Ops:
  7.2 14.8 %copy-start = (bf16[256,2048]{1,0:T(8,128)(2,1)S(1)}, bf16[256,2048]{1,0:T(8,128)(2,1)}, u32[]{:S(2)}) copy-start(bf16[256,2048]{1,0:T(8,128)(2,1)} %param.7) | copy-start | bytes 3145732
  16.8 11.1 %all-to-all-start.1 = ((bf16[8,128,8]{1,2,0:T(8,128)(2,1)}), bf16[8,128,8]{1,2,0:T(8,128)(2,1)S(1)}, u32[]{:S(2)}, u32[]{:S(2)}) async-start(bf16[8,128,8]{1,2,0:T(8,128)(2,1)} %fusion.27), calls=%async_computation.2 | async-start | bytes 32768 | tf_op jit(solution)/shard_map/all_to_all | solution.py:114
  27.9 5.5 %copy-start.1 = (bf16[256,512]{1,0:T(8,128)(2,1)S(1)}, bf16[256,512]{1,0:T(8,128)(2,1)}, u32[]{:S(2)}) copy-start(bf16[256,512]{1,0:T(8,128)(2,1)} %param.13) | copy-start | bytes 786436
  27.9 66.4 %all-to-all-start = ((bf16[8,128,2048]{2,1,0:T(8,128)(2,1)}), bf16[8,128,2048]{2,1,0:T(8,128)(2,1)}, u32[]{:S(2)}, u32[]{:S(2)}) async-start(bf16[8,128,2048]{2,1,0:T(8,128)(2,1)} %bitcast.50), calls=%async_computation.1 | async-start | bytes 8388608 | tf_op jit(solution)/shard_map/all_to_all | solution.py:113
  32.6 141.4 %all-gather.2.cloned.1.call-start = ((), (), s32[]{:S(2)}) async-start(), calls=%async_computation.6 | async-start | bytes 1310720 | tf_op jit(solution)/shard_map/all_gather | solution.py:107
  33.4 164.3 %reduce-scatter.2.cloned.1.call-start = ((), (), s32[]{:S(2)}) async-start(), calls=%async_computation.5 | async-start | bytes 2621440 | tf_op jit(solution)/shard_map/reduce_scatter | solution.py:97
  38.4 11.5 %collective-permute-start = (bf16[1,128,512]{2,1,0:T(8,128)(2,1)}, bf16[1,128,512]{2,1,0:T(8,128)(2,1)S(1)}, u32[]{:S(2)}, u32[]{:S(2)}) collective-permute-start(bf16[1,128,512]{2,1,0:T(8,128)(2,1)} %get-tuple-element.24), channel_id=1, source_target_pairs={{0,1},{1,0},{2,3},{3,2},{4,5},{5,4},{6,7},{7,6},{8,9},{9,8},{10,11... | collective-permute-start | bytes 393224 | tf_op jit(solution)/shard_map/ppermute | solution.py:67
  38.8 45.2 %collective-permute-start.1 = (bf16[1,128,512]{2,1,0:T(8,128)(2,1)}, bf16[1,128,512]{2,1,0:T(8,128)(2,1)S(1)}, u32[]{:S(2)}, u32[]{:S(2)}) collective-permute-start(bf16[1,128,512]{2,1,0:T(8,128)(2,1)} %get-tuple-element.23), channel_id=1, source_target_pairs={{0,2},{1,3},{2,0},{3,1},{4,6},{5,7},{6,4},{7,5},{8,10},{9,11},{10,... | collective-permute-start | bytes 393224 | tf_op jit(solution)/shard_map/ppermute | solution.py:67
  40.5 45.4 %collective-permute-start.2 = (bf16[1,128,512]{2,1,0:T(8,128)(2,1)}, bf16[1,128,512]{2,1,0:T(8,128)(2,1)S(1)}, u32[]{:S(2)}, u32[]{:S(2)}) collective-permute-start(bf16[1,128,512]{2,1,0:T(8,128)(2,1)} %get-tuple-element.22), channel_id=1, source_target_pairs={{0,3},{1,2},{2,1},{3,0},{4,7},{5,6},{6,5},{7,4},{8,11},{9,10},{10,... | collective-permute-start | bytes 393224 | tf_op jit(solution)/shard_map/ppermute | solution.py:67
  40.6 45.4 %collective-permute-start.3 = (bf16[1,128,512]{2,1,0:T(8,128)(2,1)}, bf16[1,128,512]{2,1,0:T(8,128)(2,1)S(1)}, u32[]{:S(2)}, u32[]{:S(2)}) collective-permute-start(bf16[1,128,512]{2,1,0:T(8,128)(2,1)} %get-tuple-element.21), channel_id=1, source_target_pairs={{0,4},{1,5},{2,6},{3,7},{4,0},{5,1},{6,2},{7,3},{8,12},{9,13},{10,... | collective-permute-start | bytes 393224 | tf_op jit(solution)/shard_map/ppermute | solution.py:67
  42.2 43.7 %collective-permute-start.4 = (bf16[1,128,512]{2,1,0:T(8,128)(2,1)S(1)}, bf16[1,128,512]{2,1,0:T(8,128)(2,1)S(1)}, u32[]{:S(2)}, u32[]{:S(2)}) collective-permute-start(bf16[1,128,512]{2,1,0:T(8,128)(2,1)S(1)} %get-tuple-element.20), channel_id=1, source_target_pairs={{0,5},{1,4},{2,7},{3,6},{4,1},{5,0},{6,3},{7,2},{8,13},{9,12},{10,... | collective-permute-start | bytes 393224 | tf_op jit(solution)/shard_map/ppermute | solution.py:67
  49.9 40.7 %collective-permute-start.5 = (bf16[1,128,512]{2,1,0:T(8,128)(2,1)S(1)}, bf16[1,128,512]{2,1,0:T(8,128)(2,1)S(1)}, u32[]{:S(2)}, u32[]{:S(2)}) collective-permute-start(bf16[1,128,512]{2,1,0:T(8,128)(2,1)S(1)} %get-tuple-element.19), channel_id=1, source_target_pairs={{0,6},{1,7},{2,4},{3,5},{4,2},{5,3},{6,0},{7,1},{8,14},{9,15},{10,... | collective-permute-start | bytes 393224 | tf_op jit(solution)/shard_map/ppermute | solution.py:67
  84.1 8.4 %collective-permute-start.6 = (bf16[1,128,512]{2,1,0:T(8,128)(2,1)S(1)}, bf16[1,128,512]{2,1,0:T(8,128)(2,1)S(1)}, u32[]{:S(2)}, u32[]{:S(2)}) collective-permute-start(bf16[1,128,512]{2,1,0:T(8,128)(2,1)S(1)} %get-tuple-element.18), channel_id=1, source_target_pairs={{0,7},{1,6},{2,5},{3,4},{4,3},{5,2},{6,1},{7,0},{8,15},{9,14},{10,... | collective-permute-start | bytes 393224 | tf_op jit(solution)/shard_map/ppermute | solution.py:67
  150.2 18.9 %all-to-all-start.2 = ((bf16[8,128,512]{2,1,0:T(8,128)(2,1)}), bf16[8,128,512]{2,1,0:T(8,128)(2,1)S(1)}, u32[]{:S(2)}, u32[]{:S(2)}) async-start(bf16[8,128,512]{2,1,0:T(8,128)(2,1)} %bitcast.56), calls=%async_computation.3 | async-start | bytes 2097152 | tf_op jit(solution)/shard_map/all_to_all | solution.py:124
  169.1 4.9 %copy-start.2 = (s32[1,8,128]{2,1,0:T(8,128)S(1)}, s32[1,8,128]{2,1,0:T(8,128)}, u32[]{:S(2)}) copy-start(s32[1,8,128]{2,1,0:T(8,128)} %param.9) | copy-start | bytes 12292
  169.1 54.0 %all-to-all-start.3 = ((bf16[8,128,2048]{2,1,0:T(8,128)(2,1)}), bf16[8,128,2048]{2,1,0:T(8,128)(2,1)}, u32[]{:S(2)}, u32[]{:S(2)}) async-start(bf16[8,128,2048]{2,1,0:T(8,128)(2,1)} %bitcast.52), calls=%async_computation.4 | async-start | bytes 8388608 | tf_op jit(solution)/shard_map/all_to_all | solution.py:144
  174.1 7.4 %copy-start.3 = (bf16[1024,128]{0,1:T(8,128)(2,1)S(1)}, bf16[1024,128]{0,1:T(8,128)(2,1)}, u32[]{:S(2)}) copy-start(bf16[1024,128]{0,1:T(8,128)(2,1)} %get-tuple-element.17) | copy-start | bytes 786436
Sparse Core Ops, SparseCore 0:
  35.0 29.5 all-gather.1
  67.0 43.4 reduce-scatter.1
